TPU v7x, 512 devices: a whole 4x8x8 slice. The times are simulated.
512 devices in a mesh: member: 32 (over z, x), wave: 16 (over y, core).
Axes of the slice: x: 4, y: 8, z: 8, core: 2. Of those that a mesh axis runs over, the one named last changes fastest.
Arguments:
- state: float32 [32, 128, 32, 640], P('member', 'wave'), may hold values from -6 to 6
- legendre: bfloat16 [128, 640, 640], P('wave'), may hold values from -0.25 to 0.25
- lat_weights: float32 [640], replicated, may hold values from 0.5 to 2
- region: int32 [4], replicated, may hold values from 0 to 2560, as said below
- sources: int32 [32], replicated, may hold values from 0 to 31, as said below
Outputs:
- new_states: float32 [32, 128, 32, 640], P('member', 'wave')
- scores: float32 [32], P('member')
Inputs may be any that keep to these rules, and one draw needn't show every extreme that they name: region[0] < region[1] bound the latitudes and region[2] < region[3] the longitudes of the region; each band covers at least half of its grid dimension; the longitude band ends at the last longitude, region[3] = 2560. `sources`: some member is the source of at least 8 slots.
All inputs are finite; a program needn't handle non-finite values.
Results may differ from a plain program's by a relative error of at most 0.0059.
Values may be sent and summed in bfloat16 or wider, within the bound.
No kernel may reach another device: no remote copies, remote signals or barrier semaphores. Data moves between devices by JAX's collectives and lax.ppermute only.
A program may use at most 128 MiB of HBM per device.

v0:
```python
import jax
import jax.numpy as jnp
from jax import lax
from jax.sharding import PartitionSpec as P

NLON = 2560
advect_rate = 2.0


def fourier_table(waves_total, points):
    wave_index = lax.broadcasted_iota(jnp.int32, (waves_total, points), 0)
    column_index = lax.broadcasted_iota(jnp.int32, (waves_total, points), 1)
    angles = (wave_index * column_index % points).astype(jnp.float32) * (2.0 * jnp.pi / points)
    return jnp.stack([jnp.cos(angles), -jnp.sin(angles)], axis=1).astype(jnp.bfloat16)


def on_device(state, legendre, lat_weights, region, sources):
    wave_count = lax.axis_size("wave")
    waves_local = legendre.shape[0]
    waves_total = waves_local * wave_count
    degrees = legendre.shape[1]
    latitudes = legendre.shape[2]
    lat_rows = latitudes // wave_count
    state_rows = state.shape[2]
    level_count = state_rows // 4
    fourier = fourier_table(waves_total, NLON)
    spectral = state[0]
    fourier_coef = jnp.einsum(
        "mrn,mnl->mrl", spectral.astype(jnp.bfloat16), legendre, preferred_element_type=jnp.float32
    )
    fourier_coef = fourier_coef.astype(jnp.bfloat16).reshape(
        waves_local, 2, 2 * level_count, latitudes
    )
    synthesis_scale = (2.0 * waves_total) ** (-0.5)
    gridded = synthesis_scale * jnp.einsum(
        "mckl,mcx->klx",
        lax.all_to_all(fourier_coef, "wave", split_axis=3, concat_axis=0, tiled=True),
        fourier,
        preferred_element_type=jnp.float32,
    )
    lat_start = lax.axis_index("wave") * lat_rows
    local_weights = lax.dynamic_slice_in_dim(lat_weights, lat_start, lat_rows)
    wind_grid = gridded[:level_count]
    temper_grid = gridded[level_count:]
    fluxes = (
        jnp.concatenate([0.5 * wind_grid * wind_grid, wind_grid * temper_grid], axis=0)
        * local_weights[None, :, None]
    )
    fluxes = fluxes.astype(jnp.bfloat16)
    lat_index = lat_start + lax.broadcasted_iota(jnp.int32, (lat_rows, 1), 0)
    lon_index = lax.broadcasted_iota(jnp.int32, (1, NLON), 1)
    in_region = (
        (lat_index >= region[0])
        & (lat_index < region[1])
        & (lon_index >= region[2])
        & (lon_index < region[3])
    )
    lowest = temper_grid[level_count - 1]
    region_part = jnp.sum(jnp.where(in_region, local_weights[:, None] * lowest * lowest, 0.0))
    region_total = lax.psum(region_part, "wave")
    every_lat = lax.broadcasted_iota(jnp.int32, (latitudes,), 0)
    lat_inside = (every_lat >= region[0]) & (every_lat < region[1])
    region_weight = jnp.sum(jnp.where(lat_inside, lat_weights, 0.0)) * (
        region[3] - region[2]
    ).astype(jnp.float32)
    scores = (region_total / region_weight).reshape(1)
    analysis_scale = NLON ** (-0.5)
    flux_coef = analysis_scale * jnp.einsum(
        "klx,mcx->mckl", fluxes, fourier, preferred_element_type=jnp.float32
    )
    flux_coef = flux_coef.astype(jnp.bfloat16)
    tendency = jnp.einsum(
        "mckl,mnl->mckn",
        lax.all_to_all(flux_coef, "wave", split_axis=0, concat_axis=3, tiled=True),
        legendre,
        preferred_element_type=jnp.float32,
    )
    wave_ids = lax.axis_index("wave") * waves_local + lax.broadcasted_iota(
        jnp.int32, (waves_local, 1, 1), 0
    )
    advection = advect_rate * wave_ids.astype(jnp.float32) / waves_total
    degree_ids = lax.broadcasted_iota(jnp.int32, (1, 1, degrees), 2).astype(jnp.float32)
    damping = 1.0 + ((degree_ids + 1.0) / degrees) ** 2
    spectral_split = spectral.reshape(waves_local, 2, 2 * level_count, degrees)
    real_part = (spectral_split[:, 0] + advection * tendency[:, 1]) / damping
    imag_part = (spectral_split[:, 1] - advection * tendency[:, 0]) / damping
    stepped = jnp.stack([real_part, imag_part], axis=1).reshape(1, waves_local, state_rows, degrees)
    source_member = sources[lax.axis_index("member")]
    shards = lax.all_gather(stepped, "member", axis=0, tiled=True)
    owners = lax.broadcasted_iota(jnp.int32, (shards.shape[0], 1, 1, 1), 0)
    cloned = jnp.sum(jnp.where(owners == source_member, shards, 0.0), axis=0, keepdims=True)
    return (cloned, scores)


def solution(mesh):
    in_specs = (P("member", "wave", None, None), P("wave", None, None), P(), P(), P())
    out_specs = (P("member", "wave", None, None), P("member"))
    return jax.shard_map(
        on_device, mesh=mesh, in_specs=in_specs, out_specs=out_specs, check_vma=False
    )
```

profile of v0, /device:TPU:1, one launch (start us, length us, event | category | flops | bytes accessed | tf_op | source)
XLA Modules:
  0.0 273.9 jit_solution(7735756794780903431)
XLA Ops:
  7.2 4.2 %convolution_convert_fusion = bf16[8,32,640]{2,1,0:T(8,128)(2,1)S(1)} fusion(bf16[8,640,640]{2,1,0:T(8,128)(2,1)} %param.6, f32[1,8,32,640]{3,2,1,0:T(8,128)} %param.5), kind=kOutput, calls=%fused_computation.24 | convolution fusion | flops 210042880 | bytes 7536640 | tf_op jit(solution)/shard_map/mrn,mnl->mrl/dot_general | solution.py:28
  11.4 3.3 %copy.16 = bf16[8,2,16,640]{2,1,0,3:T(2,128)(2,1)S(1)} copy(bf16[8,2,16,640]{3,2,1,0:T(8,128)(2,1)S(1)} %bitcast.65) | data formatting | bytes 655360 | tf_op jit(solution)/shard_map/reshape | solution.py:31
  14.7 3.4 %reshape.118 = bf16[16,2,5120]{2,1,0:T(2,128)(2,1)} reshape(bf16[640,8,2,16]{3,2,1,0:T(2,128)(2,1)S(1)} %bitcast.60) | data formatting | bytes 655360
  18.1 10.8 %all-to-all-start = ((bf16[16,2,5120]{2,1,0:T(2,128)(2,1)}), bf16[16,2,5120]{2,1,0:T(2,128)(2,1)}, u32[]{:S(2)}, u32[]{:S(2)}) async-start(bf16[16,2,5120]{2,1,0:T(2,128)(2,1)} %reshape.118), calls=%async_computation | async-start | bytes 655360 | tf_op jit(solution)/shard_map/all_to_all | solution.py:37
  29.0 6.1 %negate_convert_fusion = (bf16[128,1,2560]{2,0,1:T(8,128)(2,1)S(1)}, bf16[128,1,2560]{2,0,1:T(8,128)(2,1)}) fusion(), kind=kLoop, calls=%fused_computation.16 | loop fusion | flops 3932160 | bytes 1310720 | tf_op jit(solution)/shard_map/convert.1
  35.2 6.3 %all-to-all-done = bf16[16,2,5120]{2,1,0:T(2,128)(2,1)} async-done(((bf16[16,2,5120]{2,1,0:T(2,128)(2,1)}), bf16[16,2,5120]{2,1,0:T(2,128)(2,1)}, u32[]{:S(2)}, u32[]{:S(2)}) %all-to-all-start) | async-done | bytes 327712 | tf_op jit(solution)/shard_map/all_to_all | solution.py:37
  41.4 8.5 %reshape.119 = bf16[640,8,2,16]{3,2,1,0:T(2,128)(2,1)S(1)} reshape(bf16[16,2,5120]{2,1,0:T(2,128)(2,1)} %all-to-all-done) | data formatting | bytes 655360
  50.0 4.7 %copy.27 = bf16[8,2,16,16,40]{4,0,3,1,2:T(8,128)(2,1)} copy(bf16[8,2,16,16,40]{2,1,0,4,3:T(2,128)(2,1)S(1)} %bitcast.61) | data formatting | bytes 655360 | tf_op jit(solution)/shard_map/all_to_all | solution.py:37
  54.7 2.5 bitcast_multiply_fusion
  58.1 1.9 copy-done
  61.2 1.4 copy.20
  62.6 2.4 reshape.120
  65.0 3.6 %all-to-all-start.1 = ((bf16[16,2,5120]{2,1,0:T(2,128)(2,1)}), bf16[16,2,5120]{2,1,0:T(2,128)(2,1)S(1)}, u32[]{:S(2)}, u32[]{:S(2)}) async-start(bf16[16,2,5120]{2,1,0:T(2,128)(2,1)} %reshape.120), calls=%async_computation.1 | async-start | bytes 655360 | tf_op jit(solution)/shard_map/all_to_all | solution.py:74
  69.0 12.8 %all-to-all-done.1 = bf16[16,2,5120]{2,1,0:T(2,128)(2,1)S(1)} async-done(((bf16[16,2,5120]{2,1,0:T(2,128)(2,1)}), bf16[16,2,5120]{2,1,0:T(2,128)(2,1)S(1)}, u32[]{:S(2)}, u32[]{:S(2)}) %all-to-all-start.1) | async-done | bytes 327712 | tf_op jit(solution)/shard_map/all_to_all | solution.py:74
  81.7 1.6 reshape.121
  84.1 1.2 all_to_all.33
  85.3 4.9 %fusion.1 = f32[8,2,16,640]{3,2,1,0:T(8,128)S(1)} fusion(bf16[8,2,16,640]{3,2,1,0:T(8,128)(2,1)S(1)} %all_to_all.33, bf16[8,640,640]{2,1,0:T(8,128)(2,1)} %param.6), kind=kOutput, calls=%fused_computation.3 | convolution fusion | flops 209715200 | bytes 7536640 | tf_op jit(solution)/shard_map/mckl,mnl->mckn/dot_general | solution.py:72
  94.5 1.3 compare_and_fusion
  95.9 1.3 iota_compare_fusion
  97.1 1.9 select_reduce_fusion.1
  99.0 1.9 fusion.25
  101.5 23.4 %psum.7 = f32[]{:T(128)} all-reduce(f32[]{:T(128)} %fusion.25), channel_id=1, replica_groups=mesh['member'=32,'wave'=16] {'wave'}, use_global_device_ids=true, to_apply=%region_2.3 | all-reduce | flops 1 | bytes 8 | tf_op jit(solution)/shard_map/psum | solution.py:60
  125.5 130.8 %all-gather.2.cloned.1.call-done = f32[32,8,32,640]{3,2,1,0:T(8,128)} async-done(((f32[1,8,32,640]{3,2,1,0:T(8,128)}), f32[32,8,32,640]{3,2,1,0:T(8,128)}) %all-gather.2.cloned.1.call-update) | async-done | bytes 20971536 | tf_op jit(solution)/shard_map/all_gather | solution.py:89
  256.3 9.6 %select_reduce_fusion = f32[8,32,640]{2,1,0:T(8,128)} fusion(f32[32,8,32,640]{3,2,1,0:T(8,128)} %all-gather.2.cloned.1.call-done, pred[32]{0:T(512)(128)(4,1)S(1)} %iota_compare_fusion.4), kind=kLoop, calls=%fused_computation | loop fusion | flops 10321920 | bytes 21626912 | tf_op jit(solution)/shard_map/reduce_sum | solution.py:91
  (24 shorter events, 6.1 us)
Async XLA Ops:
  11.4 17.6 %copy-start.4 = (f32[640]{0:T(1024)S(1)}, f32[640]{0:T(1024)}, u32[]{:S(2)}) copy-start(f32[640]{0:T(1024)} %param.7) | copy-start | bytes 7684
  18.1 23.3 %all-to-all-start = ((bf16[16,2,5120]{2,1,0:T(2,128)(2,1)}), bf16[16,2,5120]{2,1,0:T(2,128)(2,1)}, u32[]{:S(2)}, u32[]{:S(2)}) async-start(bf16[16,2,5120]{2,1,0:T(2,128)(2,1)} %reshape.118), calls=%async_computation | async-start | bytes 655360 | tf_op jit(solution)/shard_map/all_to_all | solution.py:37
  57.2 2.8 %copy-start = (f32[16,40,2560]{2,1,0:T(8,128)}, f32[16,40,2560]{2,1,0:T(8,128)S(1)}, u32[]{:S(2)}) copy-start(f32[16,40,2560]{2,1,0:T(8,128)S(1)} %bitcast_multiply_fusion) | copy-start | bytes 19660804
  57.2 2.7 %copy-start.2 = (bf16[128,1,2560]{2,0,1:T(8,128)(2,1)S(1)}, bf16[128,1,2560]{2,0,1:T(8,128)(2,1)}, u32[]{:S(2)}) copy-start(bf16[128,1,2560]{2,0,1:T(8,128)(2,1)} %get-tuple-element.11) | copy-start | bytes 1966084
  65.0 16.7 %all-to-all-start.1 = ((bf16[16,2,5120]{2,1,0:T(2,128)(2,1)}), bf16[16,2,5120]{2,1,0:T(2,128)(2,1)S(1)}, u32[]{:S(2)}, u32[]{:S(2)}) async-start(bf16[16,2,5120]{2,1,0:T(2,128)(2,1)} %reshape.120), calls=%async_computation.1 | async-start | bytes 655360 | tf_op jit(solution)/shard_map/all_to_all | solution.py:74
  68.7 187.7 %all-gather.2.cloned.1.call-start = ((), (), s32[]{:S(2)}) async-start(), calls=%async_computation.2 | async-start | bytes 21626880 | tf_op jit(solution)/shard_map/all_gather | solution.py:89
  85.3 5.0 %copy-start.1 = (f32[1,8,32,640]{3,2,1,0:T(8,128)S(1)}, f32[1,8,32,640]{3,2,1,0:T(8,128)}, u32[]{:S(2)}) copy-start(f32[1,8,32,640]{3,2,1,0:T(8,128)} %param.5) | copy-start | bytes 1966084
  90.2 1.1 copy-start.3
  90.2 3.0 %copy-start.5 = (s32[32]{0:T(128)S(1)}, s32[32]{0:T(128)}, u32[]{:S(2)}) copy-start(s32[32]{0:T(128)} %param.9) | copy-start | bytes 388
Sparse Core Ops, SparseCore 0:
  91.5 164.8 all-gather.1
where the time goes:
time: 274 us
  waiting for transfers between devices  150 us (55%)
  local copies, waits for them, and re-layouts  30.6 us (11%)
  other arithmetic  24.6 us (9%)
  blocking collectives  23.4 us (9%)
  between operations  17.8 us (6%)
  starting transfers between devices  14.7 us (5%)
  matrix products  12.9 us (5%)
    all_gather x1, waiting for transfers between devices, on_device(): shards = lax.all_gather(stepped, 'member', axis=0, tiled=True)  131 us
    psum x1, blocking collectives, on_device(): region_total = lax.psum(region_part, 'wave')  23.4 us
    unnamed x16, local copies, waits for them, and re-layouts  17.9 us
    all_to_all x1, waiting for transfers between devices, on_device(): lax.all_to_all(flux_coef, 'wave', split_axis=0, concat_axis=3, tiled=True)  12.8 us
    all_to_all x1, starting transfers between devices, on_device(): lax.all_to_all(fourier_coef, 'wave', split_axis=3, concat_axis=0, tiled=T...  10.8 us
    reduce_sum x1, other arithmetic, on_device(): jnp.sum(jnp.where(owners == source_member, shards, 0.0), axis=0, keepdims...  9.6 us
    all_to_all x1, waiting for transfers between devices, on_device(): lax.all_to_all(fourier_coef, 'wave', split_axis=3, concat_axis=0, tiled=T...  6.27 us
    another operation x1, other arithmetic  6.15 us
  transfers between devices with their start and end apart: 3, of which 3 were waited for; matrix products, arithmetic and copies ran while one was open for 5% of the time, Pallas kernels for 0%

commit v1 on v0

--- a/solution.py
+++ b/solution.py
@@ -86,7 +86,9 @@
     imag_part = (spectral_split[:, 1] - advection * tendency[:, 0]) / damping
     stepped = jnp.stack([real_part, imag_part], axis=1).reshape(1, waves_local, state_rows, degrees)
     source_member = sources[lax.axis_index("member")]
-    shards = lax.all_gather(stepped, "member", axis=0, tiled=True)
+    shards = jnp.concatenate(
+        lax.all_to_all(jnp.stack([stepped] * lax.axis_size("member")), "member", 0, 0), axis=0
+    )
     owners = lax.broadcasted_iota(jnp.int32, (shards.shape[0], 1, 1, 1), 0)
     cloned = jnp.sum(jnp.where(owners == source_member, shards, 0.0), axis=0, keepdims=True)
     return (cloned, scores)

time: 274 us -> 639 us (2.33)
  the two profiles are of different devices: /device:TPU:1 before, /device:TPU:136 now
where the time goes in v1:
time: 639 us; the launch traced here: 638 us
  waiting for transfers between devices  509 us (80%)
  local copies, waits for them, and re-layouts  40.2 us (6%)
  starting transfers between devices  24.7 us (4%)
  blocking collectives  23.8 us (4%)
  other arithmetic  23.7 us (4%)
  matrix products  12.9 us (2%)
    all_to_all x1, waiting for transfers between devices, on_device(): lax.all_to_all(jnp.stack([stepped] * lax.axis_size('member')), 'member',...  493 us
    psum x1, blocking collectives, on_device(): region_total = lax.psum(region_part, 'wave')  23.8 us
    unnamed x16, local copies, waits for them, and re-layouts  17.9 us
  transfers between devices with their start and end apart: 3, of which 3 were waited for; matrix products, arithmetic and copies ran while one was open for 2% of the time, Pallas kernels for 0%

profile of v1, /device:TPU:136, one launch (start us, length us, event | category | flops | bytes accessed | tf_op | source)
XLA Modules:
  0.0 638.4 jit_solution(7231766719573247531)
XLA Ops:
  0.6 4.2 convolution_convert_fusion
  4.8 3.3 copy.16
  8.1 3.4 reshape.122
  11.6 7.6 %all-to-all-start = ((bf16[16,2,5120]{2,1,0:T(2,128)(2,1)}), bf16[16,2,5120]{2,1,0:T(2,128)(2,1)}, u32[]{:S(2)}, u32[]{:S(2)}) async-start(bf16[16,2,5120]{2,1,0:T(2,128)(2,1)} %reshape.122), calls=%async_computation | async-start | bytes 655360 | tf_op jit(solution)/shard_map/all_to_all | solution.py:37
  19.2 6.1 negate_convert_fusion
  25.4 4.6 all-to-all-done
  29.9 8.5 %reshape.123 = bf16[640,8,2,16]{3,2,1,0:T(2,128)(2,1)S(1)} reshape(bf16[16,2,5120]{2,1,0:T(2,128)(2,1)} %all-to-all-done) | data formatting | bytes 655360
  38.5 4.7 copy.27
  43.2 2.5 bitcast_multiply_fusion
  46.6 1.9 copy-done
  49.7 1.4 copy.20
  51.2 2.4 reshape.124
  53.6 5.3 all-to-all-start.1
  58.9 11.1 %all-to-all-done.1 = bf16[16,2,5120]{2,1,0:T(2,128)(2,1)S(1)} async-done(((bf16[16,2,5120]{2,1,0:T(2,128)(2,1)}), bf16[16,2,5120]{2,1,0:T(2,128)(2,1)S(1)}, u32[]{:S(2)}, u32[]{:S(2)}) %all-to-all-start.1) | async-done | bytes 327712 | tf_op jit(solution)/shard_map/all_to_all | solution.py:74
  70.0 1.6 reshape.125
  73.5 4.9 fusion.2
  78.7 9.6 %stack.16 = f32[32,1,8,32,640]{4,3,2,1,0:T(8,128)} broadcast(f32[8,32,640]{2,1,0:T(8,128)S(1)} %bitcast.68), dimensions={2,3,4} | broadcast | bytes 21626880 | tf_op jit(solution)/shard_map/stack | solution.py:90
  88.3 11.9 %all-to-all-start.2 = ((f32[32,1,8,32,640]{4,3,2,1,0:T(8,128)}), f32[32,1,8,32,640]{4,3,2,1,0:T(8,128)}, u32[]{:S(2)}, u32[]{:S(2)}) async-start(f32[32,1,8,32,640]{4,3,2,1,0:T(8,128)} %stack.16), calls=%async_computation.2 | async-start | bytes 41943040 | tf_op jit(solution)/shard_map/all_to_all | solution.py:90
  103.3 1.3 compare_and_fusion
  105.7 1.9 select_reduce_fusion
  107.7 1.9 fusion.26
  110.1 23.8 %psum.7 = f32[]{:T(128)} all-reduce(f32[]{:T(128)} %fusion.26), channel_id=1, replica_groups=mesh['member'=32,'wave'=16] {'wave'}, use_global_device_ids=true, to_apply=%region_2.3 | all-reduce | flops 1 | bytes 8 | tf_op jit(solution)/shard_map/psum | solution.py:60
  134.6 493.1 %all-to-all-done.2 = f32[32,1,8,32,640]{4,3,2,1,0:T(8,128)} async-done(((f32[32,1,8,32,640]{4,3,2,1,0:T(8,128)}), f32[32,1,8,32,640]{4,3,2,1,0:T(8,128)}, u32[]{:S(2)}, u32[]{:S(2)}) %all-to-all-start.2) | async-done | bytes 20971552 | tf_op jit(solution)/shard_map/all_to_all | solution.py:90
  627.7 9.6 %fusion = f32[8,32,640]{2,1,0:T(8,128)} fusion(f32[32,1,8,32,640]{4,3,2,1,0:T(8,128)} %all-to-all-done.2, pred[32]{0:T(512)(128)(4,1)S(1)} %iota_compare_fusion.4), kind=kLoop, calls=%fused_computation.1 | loop fusion | flops 10321920 | bytes 21626912 | tf_op jit(solution)/shard_map/reduce_sum | solution.py:93
  (24 shorter events, 7.3 us)
Async XLA Ops:
  4.8 14.3 %copy-start.4 = (f32[640]{0:T(1024)S(1)}, f32[640]{0:T(1024)}, u32[]{:S(2)}) copy-start(f32[640]{0:T(1024)} %param.7) | copy-start | bytes 7684
  11.6 18.4 %all-to-all-start = ((bf16[16,2,5120]{2,1,0:T(2,128)(2,1)}), bf16[16,2,5120]{2,1,0:T(2,128)(2,1)}, u32[]{:S(2)}, u32[]{:S(2)}) async-start(bf16[16,2,5120]{2,1,0:T(2,128)(2,1)} %reshape.122), calls=%async_computation | async-start | bytes 655360 | tf_op jit(solution)/shard_map/all_to_all | solution.py:37
  45.7 2.8 copy-start
  45.7 2.8 copy-start.2
  53.6 16.4 %all-to-all-start.1 = ((bf16[16,2,5120]{2,1,0:T(2,128)(2,1)}), bf16[16,2,5120]{2,1,0:T(2,128)(2,1)S(1)}, u32[]{:S(2)}, u32[]{:S(2)}) async-start(bf16[16,2,5120]{2,1,0:T(2,128)(2,1)} %reshape.124), calls=%async_computation.1 | async-start | bytes 655360 | tf_op jit(solution)/shard_map/all_to_all | solution.py:74
  73.5 5.0 copy-start.1
  88.3 11.9 %copy-start.3 = (s32[4]{0:T(128)S(1)}, s32[4]{0:T(128)}, u32[]{:S(2)}) copy-start(s32[4]{0:T(128)} %param.8) | copy-start | bytes 52
  88.3 13.7 %copy-start.5 = (s32[32]{0:T(128)S(1)}, s32[32]{0:T(128)}, u32[]{:S(2)}) copy-start(s32[32]{0:T(128)} %param.9) | copy-start | bytes 388
  88.3 539.3 %all-to-all-start.2 = ((f32[32,1,8,32,640]{4,3,2,1,0:T(8,128)}), f32[32,1,8,32,640]{4,3,2,1,0:T(8,128)}, u32[]{:S(2)}, u32[]{:S(2)}) async-start(f32[32,1,8,32,640]{4,3,2,1,0:T(8,128)} %stack.16), calls=%async_computation.2 | async-start | bytes 41943040 | tf_op jit(solution)/shard_map/all_to_all | solution.py:90
